TPU v7x, 512 devices: a whole 4x8x8 slice. The times are simulated.
512 devices in a mesh: query: 16 (over y, x_lo), train: 16 (over x_hi, z), mp: 2 (over core).
Axes of the slice: x: 4 (x_hi: 2, x_lo: 2; x = x_hi * 2 + x_lo), y: 8, z: 8, core: 2. Of those that a mesh axis runs over, the one named last changes fastest.
Arguments:
- residual: bfloat16 [2048, 8192], P('train'), may hold values from -6 to 6
- norm_gain: float32 [8192], replicated, may hold values from 0.1 to 1.9
- gate_weight: bfloat16 [8192, 14336], P('train', ('query', 'mp')), may hold values from -0.0625 to 0.0625
- up_weight: bfloat16 [8192, 14336], P('train', ('query', 'mp')), may hold values from -0.0625 to 0.0625
- out_grad: bfloat16 [2048, 8192], P('train', ('query', 'mp')), may hold values from -6 to 6
- left_factor: bfloat16 [32, 32, 14336], P(('query', 'mp')), may hold values from -0.0078125 to 0.0078125
- right_factor: bfloat16 [32, 32, 8192], P(('query', 'mp')), may hold values from -0.0625 to 0.0625
Outputs:
- scores: float32 [32, 2048], P(('query', 'mp'), 'train')
All inputs are finite; a program needn't handle non-finite values.
Results may differ from a plain program's by a relative error of at most 0.023.
Values may be sent and summed in bfloat16 or wider, within the bound.
No kernel may reach another device: no remote copies, remote signals or barrier semaphores. Data moves between devices by JAX's collectives and lax.ppermute only.
A program may use at most 64 MiB of HBM per device.

v0:
```python
import jax
import jax.numpy as jnp
from jax import lax
from jax.sharding import Mesh
from jax.sharding import PartitionSpec as P

TRAIN = ("train_0", "train_1")
norm_eps = 1e-05


def sum_in_order(tiles, axes, sequence):
    dims = [lax.axis_size(a) for a in axes]
    tiles = tiles.reshape(*dims, *tiles.shape[1:])
    tiles = tiles.transpose(*sequence, *range(len(axes), tiles.ndim))
    tiles = tiles.reshape(-1, *tiles.shape[len(axes) :])
    for k in sequence:
        tiles = lax.psum_scatter(tiles, axes[k], scatter_dimension=0, tiled=True)
    return tiles[0]


def split_up(value, dim, peers):
    before, after = (value.shape[:dim], value.shape[dim + 1 :])
    return jnp.moveaxis(value.reshape(*before, peers, -1, *after), dim, 0)


def summed_rows(value, axes, sequence, dim):
    peers = lax.axis_size(axes)
    return sum_in_order(split_up(value, dim, peers), axes, sequence)


def sent_to_all(value, axis):
    copies = jnp.broadcast_to(value, (lax.axis_size(axis), *value.shape))
    return lax.all_to_all(copies, axis, split_axis=0, concat_axis=0, tiled=True)


def laid_out(tiles, dim):
    dims = list(tiles.shape[1:])
    dims[dim] *= tiles.shape[0]
    return jnp.moveaxis(tiles, 0, dim).reshape(dims)


def collect(value, axis, dim):
    tiles = sent_to_all(value, axis)
    return laid_out(tiles, dim)


def on_device(residual, norm_gain, gate_weight, up_weight, out_grad, left_factor, right_factor):
    values = residual.astype(jnp.float32)
    mean_sq = jnp.mean(values * values, axis=1, keepdims=True)
    normed = (values * lax.rsqrt(mean_sq + norm_eps) * norm_gain[None, :]).astype(jnp.bfloat16)
    tok_rows = normed.shape[0]
    hidden_cols = gate_weight.shape[1]
    all_rows = lax.all_to_all(normed, TRAIN, split_axis=1, concat_axis=0, tiled=True)
    paired = jnp.concatenate([gate_weight, up_weight], axis=1)
    summed = summed_rows(
        jnp.dot(all_rows, paired, preferred_element_type=jnp.float32).astype(jnp.bfloat16),
        TRAIN,
        (1, 0),
        0,
    ).astype(jnp.float32)
    activation = (jax.nn.silu(summed[:, :hidden_cols]) * summed[:, hidden_cols:]).astype(
        jnp.bfloat16
    )
    queries = left_factor.shape[0]
    factor_rank = left_factor.shape[1]
    contract = (((1,), (1,)), ((), ()))
    left_flat = left_factor.reshape(queries * factor_rank, left_factor.shape[2])
    columns = left_flat
    projected = lax.dot_general(
        columns,
        lax.all_gather(activation, ("query", "mp"), axis=1, tiled=True),
        contract,
        preferred_element_type=jnp.float32,
    )
    right_flat = right_factor.reshape(queries * factor_rank, right_factor.shape[2])
    columns = right_flat
    sensed = lax.dot_general(
        columns, collect(out_grad, ("query", "mp"), 1), contract, preferred_element_type=jnp.float32
    )
    return jnp.sum((projected * sensed).reshape(queries, factor_rank, tok_rows), axis=1)


def solution(mesh):
    torus = Mesh(
        mesh.devices.reshape(mesh.shape["query"], 2, 8, mesh.shape["mp"]),
        ("query", "train_0", "train_1", "mp"),
    )
    placed = (
        P(TRAIN, None),
        P(),
        P(TRAIN, ("query", "mp")),
        P(TRAIN, ("query", "mp")),
        P(TRAIN, ("query", "mp")),
        P(("query", "mp"), None, None),
        P(("query", "mp"), None, None),
    )
    return jax.shard_map(
        on_device, mesh=torus, in_specs=placed, out_specs=P(("query", "mp"), TRAIN), check_vma=False
    )
```

profile of v0, /device:TPU:1, one launch (start us, length us, event | category | flops | bytes accessed | tf_op | source)
XLA Modules:
  0.0 259.8 jit_solution(11499937530667813829)
XLA Ops:
  6.5 0.0 copy-start
  6.5 0.0 reduce-scatter.3.cloned.1.call-start
  6.5 3.3 %copy.14 = bf16[128,8192]{0,1:T(8,128)(2,1)S(1)} copy(bf16[128,8192]{1,0:T(8,128)(2,1)} %param.7) | data formatting | bytes 4194304 | tf_op args[0]
  9.8 0.0 copy-start.3
  9.9 1.1 fusion
  11.0 0.0 copy-done.3
  11.0 3.5 %fusion.2 = bf16[128,8192]{0,1:T(8,128)(2,1)S(1)} fusion(bf16[128,8192]{0,1:T(8,128)(2,1)S(1)} %copy.14, f32[8192]{0:T(1024)S(1)} %copy-done.3, f32[128]{0:T(128)S(1)} %add_rsqrt_fusion), kind=kLoop, calls=%fused_computation.4 | loop fusion | flops 4194304 | bytes 4227584 | tf_op jit(solution)/shard_map/convert_element_type | solution.py:50
  14.5 62.2 %all_to_all.24 = bf16[128,16,512]{0,2,1:T(8,128)(2,1)S(1)} all-to-all(bf16[128,16,512]{0,2,1:T(8,128)(2,1)S(1)} %bitcast.31), channel_id=1, replica_groups=mesh['query'=16,'train_0'=2,'train_1'=8,'mp'=2] {'train_0','train_1'}, dimensions={1} | all-to-all | bytes 4194304 | tf_op jit(solution)/shard_map/all_to_all | solution.py:53
  76.6 0.0 copy-start.4
  76.6 2.6 %copy.15 = bf16[16,128,512]{2,1,0:T(8,128)(2,1)} copy(bf16[16,128,512]{1,2,0:T(8,128)(2,1)S(1)} %bitcast.32) | data formatting | bytes 4194304 | tf_op jit(solution)/shard_map/all_to_all | solution.py:53
  79.2 0.0 copy-done.4
  79.2 4.0 %convolution_convert_fusion = bf16[2048,896]{1,0:T(8,128)(2,1)S(1)} fusion(bf16[2048,512]{1,0:T(8,128)(2,1)} %bitcast.34, bf16[512,448]{0,1:T(8,128)(2,1)S(1)} %copy-done.4, bf16[512,448]{0,1:T(8,128)(2,1)} %param.9), kind=kOutput, calls=%fused_computation.5 | convolution fusion | flops 1882718208 | bytes 6684672 | tf_op jit(solution)/shard_map/dot_general | solution.py:56
  83.3 2.2 copy.16
  85.4 0.0 copy-start.2
  85.4 0.0 reduce-scatter.3.cloned.1.call-update
  85.4 0.0 reduce-scatter.5.cloned.1.call-start
  85.5 52.5 %reduce-scatter.3.cloned.1.call-done = bf16[2,128,896]{2,1,0:T(8,128)(2,1)} async-done(((bf16[16,128,896]{2,1,0:T(8,128)(2,1)}), bf16[2,128,896]{2,1,0:T(8,128)(2,1)}) %reduce-scatter.3.cloned.1.call-update) | async-done | bytes 458768 | tf_op jit(solution)/shard_map/reduce_scatter | solution.py:17
  138.0 0.0 reduce-scatter.5.cloned.1.call-update
  138.0 0.0 all-gather.2.cloned.1.call-start
  138.1 24.4 %reduce-scatter.5.cloned.1.call-done = bf16[1,128,896]{2,1,0:T(8,128)(2,1)} async-done(((bf16[2,128,896]{2,1,0:T(8,128)(2,1)}), bf16[1,128,896]{2,1,0:T(8,128)(2,1)}) %reduce-scatter.5.cloned.1.call-update) | async-done | bytes 229392 | tf_op jit(solution)/shard_map/reduce_scatter | solution.py:17
  162.5 1.0 bitcast_convert_fusion
  163.5 0.1 fusion.11
  163.6 0.8 copy.17
  164.4 0.0 all-gather.2.cloned.1.call-update
  164.4 0.0 copy-done.2
  164.4 0.1 copy.18
  164.5 0.5 broadcast_in_dim.2
  165.0 0.0 copy-start.1
  165.0 72.9 %all_to_all.25 = bf16[32,128,256]{1,2,0:T(8,128)(2,1)S(1)} all-to-all(bf16[32,128,256]{1,2,0:T(8,128)(2,1)S(1)} %broadcast_in_dim.2), channel_id=1, replica_groups=mesh['query'=16,'train_0'=2,'train_1'=8,'mp'=2] {'query','mp'}, dimensions={0} | all-to-all | bytes 4194304 | tf_op jit(solution)/shard_map/all_to_all | solution.py:33
  237.9 0.0 copy-done.1
  237.9 0.4 fusion.9
  238.3 11.7 %all-gather.2.cloned.1.call-done = bf16[128,14336]{0,1:T(8,128)(2,1)} async-done(((bf16[128,448]{0,1:T(8,128)(2,1)}), bf16[128,14336]{0,1:T(8,128)(2,1)}) %all-gather.2.cloned.1.call-update) | async-done | bytes 3670032 | tf_op jit(solution)/shard_map/all_gather | solution.py:71
  250.0 0.0 copy-done
  250.0 3.2 %fusion.4 = f32[128]{0:T(128)} fusion(f32[32,128]{1,0:T(8,128)S(1)} %fusion.9, bf16[128,14336]{0,1:T(8,128)(2,1)} %all-gather.2.cloned.1.call-done, bf16[1,32,14336]{2,1,0:T(8,128)(2,1)S(1)} %copy-done), kind=kOutput, calls=%fused_computation.8 | convolution fusion | flops 117448576 | bytes 4604416 | tf_op jit(solution)/shard_map/dot_general | solution.py:69
  (1 shorter events, 0.0 us)
Async XLA Ops:
  6.5 243.5 %copy-start = (bf16[1,32,14336]{2,1,0:T(8,128)(2,1)S(1)}, bf16[1,32,14336]{2,1,0:T(8,128)(2,1)}, u32[]{:S(2)}) copy-start(bf16[1,32,14336]{2,1,0:T(8,128)(2,1)} %param.12) | copy-start | bytes 2752516
  6.5 131.5 %reduce-scatter.3.cloned.1.call-start = ((), (), s32[]{:S(2)}) async-start(), calls=%async_computation.4 | async-start | bytes 4128768 | tf_op jit(solution)/shard_map/reduce_scatter | solution.py:17
  9.8 1.1 copy-start.3
  76.6 2.6 %copy-start.4 = (bf16[512,448]{0,1:T(8,128)(2,1)S(1)}, bf16[512,448]{0,1:T(8,128)(2,1)}, u32[]{:S(2)}) copy-start(bf16[512,448]{0,1:T(8,128)(2,1)} %param.10) | copy-start | bytes 1376260
  85.4 79.0 %copy-start.2 = (bf16[128,256]{1,0:T(8,128)(2,1)S(1)}, bf16[128,256]{1,0:T(8,128)(2,1)}, u32[]{:S(2)}) copy-start(bf16[128,256]{1,0:T(8,128)(2,1)} %param.11) | copy-start | bytes 196612
  85.4 77.0 %reduce-scatter.5.cloned.1.call-start = ((), (), s32[]{:S(2)}) async-start(), calls=%async_computation.5 | async-start | bytes 688128 | tf_op jit(solution)/shard_map/reduce_scatter | solution.py:17
  138.0 112.0 %all-gather.2.cloned.1.call-start = ((), (), s32[]{:S(2)}) async-start(), calls=%async_computation.6 | async-start | bytes 3784704 | tf_op jit(solution)/shard_map/all_gather | solution.py:71
  165.0 72.9 %copy-start.1 = (bf16[1,32,8192]{2,1,0:T(8,128)(2,1)S(1)}, bf16[1,32,8192]{2,1,0:T(8,128)(2,1)}, u32[]{:S(2)}) copy-start(bf16[1,32,8192]{2,1,0:T(8,128)(2,1)} %param.13) | copy-start | bytes 1572868
Sparse Core Ops, SparseCore 0:
  85.6 52.3 reduce-scatter.2
  140.8 21.6 reduce-scatter.4
  164.9 85.1 all-gather.1
where the time goes:
time: 260 us
  blocking collectives  135 us (52%)
  waiting for transfers between devices  88.6 us (34%)
  between operations  13.2 us (5%)
  local copies, waits for them, and re-layouts  9.42 us (4%)
  matrix products  7.71 us (3%)
  other arithmetic  5.69 us (2%)
    reduce_scatter x2, waiting for transfers between devices, sum_in_order(): tiles = lax.psum_scatter(tiles, axes[k], scatter_dimension=0, tiled=True)  76.9 us
    all_to_all x1, blocking collectives, sent_to_all(): return lax.all_to_all(copies, axis, split_axis=0, concat_axis=0, tiled=True)  72.9 us
    all_to_all x1, blocking collectives, on_device(): lax.all_to_all(normed, TRAIN, split_axis=1, concat_axis=0, tiled=True)  62.2 us
    all_gather x1, waiting for transfers between devices, on_device(): lax.all_gather(activation, ('query', 'mp'), axis=1, tiled=True)  11.7 us
  transfers between devices with their start and end apart: 3, of which 3 were waited for; matrix products, arithmetic and copies ran while one was open for 0% of the time, Pallas kernels for 0%

commit v1 on v0

--- a/solution.py
+++ b/solution.py
@@ -50,7 +50,10 @@
     normed = (values * lax.rsqrt(mean_sq + norm_eps) * norm_gain[None, :]).astype(jnp.bfloat16)
     tok_rows = normed.shape[0]
     hidden_cols = gate_weight.shape[1]
-    all_rows = lax.all_to_all(normed, TRAIN, split_axis=1, concat_axis=0, tiled=True)
+    all_rows = jnp.concatenate(
+        lax.all_to_all(jnp.stack(jnp.split(normed, lax.axis_size(TRAIN), axis=1)), TRAIN, 0, 0),
+        axis=0,
+    )
     paired = jnp.concatenate([gate_weight, up_weight], axis=1)
     summed = summed_rows(
         jnp.dot(all_rows, paired, preferred_element_type=jnp.float32).astype(jnp.bfloat16),

time: 260 us -> 252 us (0.969)
  local copies, waits for them, and re-layouts: 9.42 us -> 3.77 us
    unnamed x12 -> x28, local copies, waits for them, and re-layouts: 3.43 us -> 0.37 us
    all_to_all x1 -> x0, local copies, waits for them, and re-layouts: 2.6 us -> none  [on_device(): lax.all_to_all(normed, TRAIN, split_axis=1, concat_axis=0, tiled=True)]
where the time goes in v1:
time: 252 us
  blocking collectives  135 us (54%)
  waiting for transfers between devices  88.8 us (35%)
  between operations  13.3 us (5%)
  matrix products  6.07 us (2%)
  other arithmetic  4.74 us (2%)
  local copies, waits for them, and re-layouts  3.77 us (1%)
    reduce_scatter x2, waiting for transfers between devices, sum_in_order(): tiles = lax.psum_scatter(tiles, axes[k], scatter_dimension=0, tiled=True)  76.9 us
    all_to_all x1, blocking collectives, sent_to_all(): return lax.all_to_all(copies, axis, split_axis=0, concat_axis=0, tiled=True)  72.9 us
    all_to_all x1, blocking collectives, on_device(): lax.all_to_all(jnp.stack(jnp.split(normed, lax.axis_size(TRAIN), axis=1))...  62.3 us
    all_gather x1, waiting for transfers between devices, on_device(): lax.all_gather(activation, ('query', 'mp'), axis=1, tiled=True)  11.8 us
  transfers between devices with their start and end apart: 3, of which 3 were waited for; matrix products, arithmetic and copies ran while one was open for 0% of the time, Pallas kernels for 0%

profile of v1, /device:TPU:1, one launch (start us, length us, event | category | flops | bytes accessed | tf_op | source)
XLA Modules:
  0.0 251.9 jit_solution(3953900544275180442)
XLA Ops:
  6.5 0.0 copy-start
  6.5 0.0 copy-start.1
  6.5 0.0 reduce-scatter.3.cloned.1.call-start
  6.5 2.2 fusion
  8.8 0.1 copy-done.1
  8.8 1.4 fusion.2
  10.5 0.0 copy-start.4
  10.6 0.0 copy-start.5
  10.6 62.3 %all_to_all.10 = bf16[16,128,512]{2,1,0:T(8,128)(2,1)S(1)} all-to-all(bf16[16,128,512]{2,1,0:T(8,128)(2,1)S(1)} %fusion.12), channel_id=1, replica_groups=mesh['query'=16,'train_0'=2,'train_1'=8,'mp'=2] {'train_0','train_1'}, dimensions={0} | all-to-all | bytes 4194304 | tf_op jit(solution)/shard_map/all_to_all | solution.py:54
  72.9 0.0 copy-done.4
  72.9 0.0 copy-done.5
  72.9 2.4 convolution_convert_fusion
  75.3 2.2 copy.10
  77.4 0.0 copy-start.3
  77.4 0.0 reduce-scatter.3.cloned.1.call-update
  77.4 0.0 reduce-scatter.5.cloned.1.call-start
  77.5 52.5 %reduce-scatter.3.cloned.1.call-done = bf16[2,128,896]{2,1,0:T(8,128)(2,1)} async-done(((bf16[16,128,896]{2,1,0:T(8,128)(2,1)}), bf16[2,128,896]{2,1,0:T(8,128)(2,1)}) %reduce-scatter.3.cloned.1.call-update) | async-done | bytes 458768 | tf_op jit(solution)/shard_map/reduce_scatter | solution.py:17
  130.0 0.0 reduce-scatter.5.cloned.1.call-update
  130.0 0.0 all-gather.2.cloned.1.call-start
  130.1 24.4 %reduce-scatter.5.cloned.1.call-done = bf16[1,128,896]{2,1,0:T(8,128)(2,1)} async-done(((bf16[2,128,896]{2,1,0:T(8,128)(2,1)}), bf16[1,128,896]{2,1,0:T(8,128)(2,1)}) %reduce-scatter.5.cloned.1.call-update) | async-done | bytes 229392 | tf_op jit(solution)/shard_map/reduce_scatter | solution.py:17
  154.5 1.0 bitcast_convert_fusion
  155.5 0.1 fusion.11
  155.6 0.8 copy.11
  156.4 0.0 all-gather.2.cloned.1.call-update
  156.4 0.0 copy-done.3
  156.4 0.1 copy.12
  156.5 0.5 broadcast_in_dim.2
  157.0 0.0 copy-start.2
  157.0 72.9 %all_to_all.11 = bf16[32,128,256]{1,2,0:T(8,128)(2,1)S(1)} all-to-all(bf16[32,128,256]{1,2,0:T(8,128)(2,1)S(1)} %broadcast_in_dim.2), channel_id=1, replica_groups=mesh['query'=16,'train_0'=2,'train_1'=8,'mp'=2] {'query','mp'}, dimensions={0} | all-to-all | bytes 4194304 | tf_op jit(solution)/shard_map/all_to_all | solution.py:33
  229.9 0.0 copy-done.2
  229.9 0.4 fusion.9
  230.4 11.8 %all-gather.2.cloned.1.call-done = bf16[128,14336]{0,1:T(8,128)(2,1)} async-done(((bf16[128,448]{0,1:T(8,128)(2,1)}), bf16[128,14336]{0,1:T(8,128)(2,1)}) %all-gather.2.cloned.1.call-update) | async-done | bytes 3670032 | tf_op jit(solution)/shard_map/all_gather | solution.py:74
  242.2 0.0 copy-done
  242.2 3.2 %fusion.4 = f32[128]{0:T(128)} fusion(f32[32,128]{1,0:T(8,128)S(1)} %fusion.9, bf16[128,14336]{0,1:T(8,128)(2,1)} %all-gather.2.cloned.1.call-done, bf16[1,32,14336]{2,1,0:T(8,128)(2,1)S(1)} %copy-done), kind=kOutput, calls=%fused_computation.8 | convolution fusion | flops 117448576 | bytes 4604416 | tf_op jit(solution)/shard_map/dot_general | solution.py:72
  (17 shorter events, 0.2 us)
Async XLA Ops:
  6.5 235.6 %copy-start = (bf16[1,32,14336]{2,1,0:T(8,128)(2,1)S(1)}, bf16[1,32,14336]{2,1,0:T(8,128)(2,1)}, u32[]{:S(2)}) copy-start(bf16[1,32,14336]{2,1,0:T(8,128)(2,1)} %param.12) | copy-start | bytes 2752516
  6.5 2.3 copy-start.1
  6.5 123.5 %reduce-scatter.3.cloned.1.call-start = ((), (), s32[]{:S(2)}) async-start(), calls=%async_computation.4 | async-start | bytes 4128768 | tf_op jit(solution)/shard_map/reduce_scatter | solution.py:17
  10.5 62.3 %copy-start.4 = (bf16[512,448]{0,1:T(8,128)(2,1)S(1)}, bf16[512,448]{0,1:T(8,128)(2,1)}, u32[]{:S(2)}) copy-start(bf16[512,448]{0,1:T(8,128)(2,1)} %param.10) | copy-start | bytes 1376260
  10.6 62.3 %copy-start.5 = (bf16[512,448]{0,1:T(8,128)(2,1)S(1)}, bf16[512,448]{0,1:T(8,128)(2,1)}, u32[]{:S(2)}) copy-start(bf16[512,448]{0,1:T(8,128)(2,1)} %param.9) | copy-start | bytes 1376260
  77.4 79.0 %copy-start.3 = (bf16[128,256]{1,0:T(8,128)(2,1)S(1)}, bf16[128,256]{1,0:T(8,128)(2,1)}, u32[]{:S(2)}) copy-start(bf16[128,256]{1,0:T(8,128)(2,1)} %param.11) | copy-start | bytes 196612
  77.4 77.1 %reduce-scatter.5.cloned.1.call-start = ((), (), s32[]{:S(2)}) async-start(), calls=%async_computation.5 | async-start | bytes 688128 | tf_op jit(solution)/shard_map/reduce_scatter | solution.py:17
  130.0 112.1 %all-gather.2.cloned.1.call-start = ((), (), s32[]{:S(2)}) async-start(), calls=%async_computation.6 | async-start | bytes 3784704 | tf_op jit(solution)/shard_map/all_gather | solution.py:74
  157.0 72.9 %copy-start.2 = (bf16[1,32,8192]{2,1,0:T(8,128)(2,1)S(1)}, bf16[1,32,8192]{2,1,0:T(8,128)(2,1)}, u32[]{:S(2)}) copy-start(bf16[1,32,8192]{2,1,0:T(8,128)(2,1)} %param.13) | copy-start | bytes 1572868
Sparse Core Ops, SparseCore 0:
  77.6 52.3 reduce-scatter.2
  132.8 21.6 reduce-scatter.4
  156.9 85.2 all-gather.1

commit v2 on v0

--- a/solution.py
+++ b/solution.py
@@ -68,7 +68,12 @@
     columns = left_flat
     projected = lax.dot_general(
         columns,
-        lax.all_gather(activation, ("query", "mp"), axis=1, tiled=True),
+        jnp.concatenate(
+            lax.all_to_all(
+                jnp.stack([activation] * lax.axis_size(("query", "mp"))), ("query", "mp"), 0, 0
+            ),
+            axis=1,
+        ),
         contract,
         preferred_element_type=jnp.float32,
     )

time: 260 us -> 270 us (1.038)
  blocking collectives: 135 us -> 62.2 us
  waiting for transfers between devices: 88.6 us -> 149 us
  starting transfers between devices: 0.08 us -> 18 us
  local copies, waits for them, and re-layouts: 9.42 us -> 13.6 us
    all_to_all x0 -> x2, waiting for transfers between devices: none -> 84.9 us  [the longest x1 84.9 us: on_device(): lax.all_to_all(jnp.stack([activation] * lax.axis_size(('query', 'mp'))),...]
    all_to_all x1 -> x0, blocking collectives: 72.9 us -> none  [sent_to_all(): return lax.all_to_all(copies, axis, split_axis=0, concat_axis=0, tiled=True)]
    all_to_all x0 -> x2, starting transfers between devices: none -> 18 us  [the longest x1 10.2 us: sent_to_all(): return lax.all_to_all(copies, axis, split_axis=0, concat_axis=0, tiled=True)]
    reduce_scatter x2, waiting for transfers between devices: 76.9 us -> 64 us  [sum_in_order(): tiles = lax.psum_scatter(tiles, axes[k], scatter_dimension=0, tiled=True)]
    all_gather x1 -> x0, waiting for transfers between devices: 11.7 us -> none  [on_device(): lax.all_gather(activation, ('query', 'mp'), axis=1, tiled=True)]
  transfers between devices with their start and end apart: 3 -> 4, of which waited for: 3 -> 3; matrix products, arithmetic and copies ran while one was open for 0% -> 1% of each run, Pallas kernels for 0% -> 0%
where the time goes in v2:
time: 270 us
  waiting for transfers between devices  149 us (55%)
  blocking collectives  62.2 us (23%)
  starting transfers between devices  18 us (7%)
  local copies, waits for them, and re-layouts  13.6 us (5%)
  between operations  13.5 us (5%)
  matrix products  7.71 us (3%)
  other arithmetic  5.69 us (2%)
    all_to_all x1, waiting for transfers between devices, on_device(): lax.all_to_all(jnp.stack([activation] * lax.axis_size(('query', 'mp'))),...  84.9 us
    reduce_scatter x2, waiting for transfers between devices, sum_in_order(): tiles = lax.psum_scatter(tiles, axes[k], scatter_dimension=0, tiled=True)  64 us
    all_to_all x1, blocking collectives, on_device(): lax.all_to_all(normed, TRAIN, split_axis=1, concat_axis=0, tiled=True)  62.2 us
    all_to_all x1, starting transfers between devices, sent_to_all(): return lax.all_to_all(copies, axis, split_axis=0, concat_axis=0, tiled=True)  10.2 us
    all_to_all x1, starting transfers between devices, on_device(): lax.all_to_all(jnp.stack([activation] * lax.axis_size(('query', 'mp'))),...  7.75 us
  transfers between devices with their start and end apart: 4, of which 3 were waited for; matrix products, arithmetic and copies ran while one was open for 1% of the time, Pallas kernels for 0%

profile of v2, /device:TPU:1, one launch (start us, length us, event | category | flops | bytes accessed | tf_op | source)
XLA Modules:
  0.0 269.7 jit_solution(3110025535996543212)
XLA Ops:
  6.5 0.0 copy-start
  6.5 0.0 reduce-scatter.3.cloned.1.call-start
  6.5 3.3 %copy.11 = bf16[128,8192]{0,1:T(8,128)(2,1)S(1)} copy(bf16[128,8192]{1,0:T(8,128)(2,1)} %param.7) | data formatting | bytes 4194304 | tf_op args[0]
  9.8 0.0 copy-start.3
  9.9 1.1 fusion
  11.0 0.0 copy-done.3
  11.0 3.5 %fusion.2 = bf16[128,8192]{0,1:T(8,128)(2,1)S(1)} fusion(bf16[128,8192]{0,1:T(8,128)(2,1)S(1)} %copy.11, f32[8192]{0:T(1024)S(1)} %copy-done.3, f32[128]{0:T(128)S(1)} %add_rsqrt_fusion), kind=kLoop, calls=%fused_computation.4 | loop fusion | flops 4194304 | bytes 4227584 | tf_op jit(solution)/shard_map/convert_element_type | solution.py:50
  14.5 62.2 %all_to_all.29 = bf16[128,16,512]{0,2,1:T(8,128)(2,1)S(1)} all-to-all(bf16[128,16,512]{0,2,1:T(8,128)(2,1)S(1)} %bitcast.34), channel_id=1, replica_groups=mesh['query'=16,'train_0'=2,'train_1'=8,'mp'=2] {'train_0','train_1'}, dimensions={1} | all-to-all | bytes 4194304 | tf_op jit(solution)/shard_map/all_to_all | solution.py:53
  76.6 0.0 copy-start.4
  76.6 2.6 copy.12
  79.2 0.0 copy-done.4
  79.2 4.0 %convolution_convert_fusion = bf16[2048,896]{1,0:T(8,128)(2,1)S(1)} fusion(bf16[2048,512]{1,0:T(8,128)(2,1)} %bitcast.37, bf16[512,448]{0,1:T(8,128)(2,1)S(1)} %copy-done.4, bf16[512,448]{0,1:T(8,128)(2,1)} %param.9), kind=kOutput, calls=%fused_computation.5 | convolution fusion | flops 1882718208 | bytes 6684672 | tf_op jit(solution)/shard_map/dot_general | solution.py:56
  83.2 2.2 copy.13
  85.4 0.0 copy-start.2
  85.4 0.0 reduce-scatter.3.cloned.1.call-update
  85.4 0.8 copy-done.2
  86.2 0.1 copy.15
  86.4 1.8 broadcast_in_dim.2
  88.2 10.2 %all-to-all-start.2 = ((bf16[32,128,256]{1,2,0:T(8,128)(2,1)}), bf16[32,128,256]{1,2,0:T(8,128)(2,1)S(1)}, u32[]{:S(2)}, u32[]{:S(2)}) async-start(bf16[32,128,256]{1,2,0:T(8,128)(2,1)} %broadcast_in_dim.2), calls=%async_computation.4 | async-start | bytes 4194304 | tf_op jit(solution)/shard_map/all_to_all | solution.py:33
  98.4 0.0 reduce-scatter.5.cloned.1.call-start
  98.4 39.6 %reduce-scatter.3.cloned.1.call-done = bf16[2,128,896]{2,1,0:T(8,128)(2,1)} async-done(((bf16[16,128,896]{2,1,0:T(8,128)(2,1)}), bf16[2,128,896]{2,1,0:T(8,128)(2,1)}) %reduce-scatter.3.cloned.1.call-update) | async-done | bytes 458768 | tf_op jit(solution)/shard_map/reduce_scatter | solution.py:17
  138.0 0.0 reduce-scatter.5.cloned.1.call-update
  138.0 24.5 %reduce-scatter.5.cloned.1.call-done = bf16[1,128,896]{2,1,0:T(8,128)(2,1)} async-done(((bf16[2,128,896]{2,1,0:T(8,128)(2,1)}), bf16[1,128,896]{2,1,0:T(8,128)(2,1)}) %reduce-scatter.5.cloned.1.call-update) | async-done | bytes 229392 | tf_op jit(solution)/shard_map/reduce_scatter | solution.py:17
  162.5 1.0 bitcast_convert_fusion
  163.5 0.1 fusion.11
  163.6 0.1 copy.14
  163.7 0.0 all-to-all-done.2
  163.8 2.7 stack.2
  166.4 0.0 copy-start.1
  166.4 7.8 %all-to-all-start.1 = ((bf16[32,128,448]{1,2,0:T(8,128)(2,1)}), bf16[32,128,448]{1,2,0:T(8,128)(2,1)}, u32[]{:S(2)}, u32[]{:S(2)}) async-start(bf16[32,128,448]{1,2,0:T(8,128)(2,1)} %stack.2), calls=%async_computation.3 | async-start | bytes 7340032 | tf_op jit(solution)/shard_map/all_to_all | solution.py:72
  174.2 0.0 copy-done.1
  174.2 0.4 fusion.9
  174.6 84.9 %all-to-all-done.1 = bf16[32,128,448]{1,2,0:T(8,128)(2,1)} async-done(((bf16[32,128,448]{1,2,0:T(8,128)(2,1)}), bf16[32,128,448]{1,2,0:T(8,128)(2,1)}, u32[]{:S(2)}, u32[]{:S(2)}) %all-to-all-start.1) | async-done | bytes 3670048 | tf_op jit(solution)/shard_map/all_to_all | solution.py:72
  259.6 0.0 copy-done
  259.6 3.2 %fusion.4 = f32[128]{0:T(128)} fusion(f32[32,128]{1,0:T(8,128)S(1)} %fusion.9, bf16[128,14336]{0,1:T(8,128)(2,1)} %bitcast.9, bf16[1,32,14336]{2,1,0:T(8,128)(2,1)S(1)} %copy-done), kind=kOutput, calls=%fused_computation.8 | convolution fusion | flops 117448576 | bytes 4604416 | tf_op jit(solution)/shard_map/dot_general | solution.py:69
  (1 shorter events, 0.0 us)
Async XLA Ops:
  6.5 253.0 %copy-start = (bf16[1,32,14336]{2,1,0:T(8,128)(2,1)S(1)}, bf16[1,32,14336]{2,1,0:T(8,128)(2,1)}, u32[]{:S(2)}) copy-start(bf16[1,32,14336]{2,1,0:T(8,128)(2,1)} %param.12) | copy-start | bytes 2752516
  6.5 131.5 %reduce-scatter.3.cloned.1.call-start = ((), (), s32[]{:S(2)}) async-start(), calls=%async_computation.5 | async-start | bytes 4128768 | tf_op jit(solution)/shard_map/reduce_scatter | solution.py:17
  9.8 1.1 copy-start.3
  76.6 2.6 copy-start.4
  85.4 0.8 copy-start.2
  88.2 75.6 %all-to-all-start.2 = ((bf16[32,128,256]{1,2,0:T(8,128)(2,1)}), bf16[32,128,256]{1,2,0:T(8,128)(2,1)S(1)}, u32[]{:S(2)}, u32[]{:S(2)}) async-start(bf16[32,128,256]{1,2,0:T(8,128)(2,1)} %broadcast_in_dim.2), calls=%async_computation.4 | async-start | bytes 4194304 | tf_op jit(solution)/shard_map/all_to_all | solution.py:33
  98.4 64.1 %reduce-scatter.5.cloned.1.call-start = ((), (), s32[]{:S(2)}) async-start(), calls=%async_computation.6 | async-start | bytes 688128 | tf_op jit(solution)/shard_map/reduce_scatter | solution.py:17
  166.4 7.8 %copy-start.1 = (bf16[1,32,8192]{2,1,0:T(8,128)(2,1)S(1)}, bf16[1,32,8192]{2,1,0:T(8,128)(2,1)}, u32[]{:S(2)}) copy-start(bf16[1,32,8192]{2,1,0:T(8,128)(2,1)} %param.13) | copy-start | bytes 1572868
  166.4 93.2 %all-to-all-start.1 = ((bf16[32,128,448]{1,2,0:T(8,128)(2,1)}), bf16[32,128,448]{1,2,0:T(8,128)(2,1)}, u32[]{:S(2)}, u32[]{:S(2)}) async-start(bf16[32,128,448]{1,2,0:T(8,128)(2,1)} %stack.2), calls=%async_computation.3 | async-start | bytes 7340032 | tf_op jit(solution)/shard_map/all_to_all | solution.py:72
Sparse Core Ops, SparseCore 0:
  85.5 52.4 reduce-scatter.2
  140.8 21.6 reduce-scatter.4
